TPU v7x, 32 devices: a whole 2x2x4 slice. The times are simulated.
32 devices in a mesh: grp: 2 (over x), seq: 16 (over z, y, core).
Axes of the slice: x: 2, y: 2, z: 4, core: 2. Of those that a mesh axis runs over, the one named last changes fastest.
Arguments:
- image_qkv: bfloat16 [3, 8, 16, 896, 128], P(None, 'grp', None, 'seq'), parts along dimension 1, may hold values from -16 to 16
- text_kv: bfloat16 [2, 2, 8, 16, 512, 128], P(None, None, 'grp', None, 'seq'), parts along dimension 2, may hold values from -6 to 6
- prompt_ids: int32 [2, 8, 512], P(None, 'grp'), parts along dimension 1, may hold values from 0 to 32127, as said below
- timesteps: int32 [8], P('grp'), parts along dimension 0, may hold values from 0 to 999
- image_states: bfloat16 [8, 896, 1536], P('grp', 'seq'), parts along dimension 0, may hold values from -6 to 6
- frozen_out: bfloat16 [2048, 1536], P('seq'), may hold values from -0.125 to 0.125
- trainee_out: bfloat16 [4096, 1536], P(('grp', 'seq')), parts along dimension 0, may hold values from -0.125 to 0.125
- time_mod: bfloat16 [256, 3072], replicated, may hold values from -0.375 to 0.375
- final_head: bfloat16 [1536, 64], replicated, may hold values from -0.15625 to 0.15625
Outputs:
- weight_grad: float32 [4096, 1536], P(('grp', 'seq')), parts along dimension 0
There are 2 independent parts, one for each index of `grp`. A program takes and returns all parts, laid end to end along the dimension named above; an argument that names none is the same for every part. Nothing has to cross between parts.
Inputs may be any that keep to these rules, and one draw needn't show every extreme that they name: `prompt_ids`: zero marks padding; in each row of 512 ids the padding is a suffix and position 0 is never padding.
All inputs are finite; a program needn't handle non-finite values.
Results may differ from a plain program's by a relative error of at most 0.011.
Values may be sent and summed in bfloat16 or wider, within the bound.
No kernel may reach another device: no remote copies, remote signals or barrier semaphores. Data moves between devices by JAX's collectives and lax.ppermute only.
A program may use at most 128 MiB of HBM per device.

v0:
```python
import math
import jax
import jax.numpy as jnp
from jax import lax
from jax.sharding import PartitionSpec as P

SAMPLES = 4
HEADS = 16
HEAD_DIM = 128
WIDTH = 1536
TIME_DIM = 256


def image_block(queries, image_keys, image_values):
    factor = HEAD_DIM ** (-0.5)
    image_scores = jnp.dot(queries, image_keys.T, preferred_element_type=jnp.float32) * factor
    image_max = jnp.max(image_scores, axis=1, keepdims=True)
    image_exp = jnp.exp(image_scores - image_max)
    image_total = jnp.sum(image_exp, axis=1, keepdims=True)
    image_part = jnp.dot(
        image_exp.astype(jnp.bfloat16), image_values, preferred_element_type=jnp.float32
    )
    return (image_max, image_total, image_part)


def text_finish(queries, image_stats, text_keys, text_values, allowed_text):
    factor = HEAD_DIM ** (-0.5)
    image_max, image_total, image_part = image_stats
    text_scores = jnp.dot(queries, text_keys.T, preferred_element_type=jnp.float32) * factor
    text_scores = jnp.where(allowed_text[None, :], text_scores, -jnp.inf)
    pass_max = jnp.maximum(image_max, jnp.max(text_scores, axis=1, keepdims=True))
    ratio = jnp.exp(image_max - pass_max)
    text_exp = jnp.exp(text_scores - pass_max)
    text_part = jnp.dot(
        text_exp.astype(jnp.bfloat16), text_values, preferred_element_type=jnp.float32
    )
    numer = ratio * image_part + text_part
    denom = ratio * image_total + jnp.sum(text_exp, axis=1, keepdims=True)
    return (numer / denom).astype(jnp.bfloat16)


def head_out(branch, states, gate, scale, final_head):
    mixed = states.astype(jnp.float32) + gate[:, None, :] * branch
    normed = (
        mixed
        * lax.rsqrt(jnp.mean(mixed * mixed, axis=-1, keepdims=True) + 1e-06)
        * (1.0 + scale[:, None, :])
    )
    normed = normed.astype(jnp.bfloat16)
    return jnp.einsum("bic,cd->bid", normed, final_head, preferred_element_type=jnp.float32)


def shards(
    image_qkv,
    text_kv,
    prompt_ids,
    timesteps,
    image_states,
    frozen_out,
    trainee_out,
    time_mod,
    final_head,
):
    group_size = lax.axis_size("seq")
    position = lax.axis_index("seq")
    image_dev = image_qkv.shape[3]
    text_dev = text_kv.shape[4]
    item_count = SAMPLES * HEADS
    owned_count = item_count // group_size
    token_rows = SAMPLES * image_dev
    image_all = image_dev * group_size
    block_rows = image_dev * min(group_size, 8)
    block_count = image_all // block_rows
    image_local = image_qkv.transpose(0, 2, 1, 3, 4).reshape(3, item_count, image_dev, HEAD_DIM)
    text_local = text_kv.transpose(0, 1, 3, 2, 4, 5).reshape(4, item_count, text_dev, HEAD_DIM)
    image_heads, text_heads = (
        lax.all_to_all(image_local, "seq", split_axis=1, concat_axis=2, tiled=True),
        lax.all_to_all(text_local, "seq", split_axis=1, concat_axis=2, tiled=True),
    )
    owned_items = position * owned_count + jnp.arange(owned_count, dtype=jnp.int32)
    sample_of = owned_items % SAMPLES
    selector = (sample_of[:, None] == jnp.arange(SAMPLES, dtype=jnp.int32)[None, :]).astype(
        jnp.float32
    )
    live_all = (prompt_ids != 0).astype(jnp.float32)
    live_owned = jnp.einsum("jb,pbt->pjt", selector, live_all) > 0.5

    def query_blocks(item_index):
        return image_heads[0, item_index].reshape(block_count, block_rows, HEAD_DIM)

    def joint_item(item_index):
        image_keys = image_heads[1, item_index]
        image_values = image_heads[2, item_index]

        def per_block(queries):
            stats = image_block(queries, image_keys, image_values)
            concept = text_finish(
                queries,
                stats,
                text_heads[0, item_index],
                text_heads[1, item_index],
                live_owned[0, item_index],
            )
            null = text_finish(
                queries,
                stats,
                text_heads[2, item_index],
                text_heads[3, item_index],
                live_owned[1, item_index],
            )
            return jnp.stack([concept, null])

        blocks = lax.map(per_block, query_blocks(item_index))
        return blocks.transpose(1, 0, 2, 3).reshape(2, image_all, HEAD_DIM)

    both_passes = lax.map(joint_item, jnp.arange(owned_count, dtype=jnp.int32)).transpose(
        1, 0, 2, 3
    )
    returned = lax.all_to_all(both_passes, "seq", split_axis=2, concat_axis=1, tiled=True)
    attention = returned.reshape(2, HEADS, SAMPLES, image_dev, HEAD_DIM).transpose(0, 2, 3, 1, 4)
    attention = attention.reshape(2, token_rows, HEADS * HEAD_DIM)
    half_dim = TIME_DIM // 2
    freqs = jnp.exp(-math.log(10000.0) * jnp.arange(half_dim, dtype=jnp.float32) / half_dim)
    angles = timesteps.astype(jnp.float32)[:, None] * freqs[None, :]
    embedding = jnp.concatenate([jnp.cos(angles), jnp.sin(angles)], 1)
    modulation = jnp.dot(embedding, time_mod.astype(jnp.float32), precision=lax.Precision.HIGHEST)
    gate = modulation[:, :WIDTH]
    scale = modulation[:, WIDTH:]
    piece_frozen = lax.all_gather(frozen_out, "seq", axis=0, tiled=True)
    piece_trainee = lax.all_gather(trainee_out, "seq", axis=0, tiled=True)
    columns_c = attention[0]
    columns_n = attention[1]
    branch_c = jnp.dot(columns_c, piece_frozen, preferred_element_type=jnp.float32)
    branch_n = jnp.dot(columns_n, piece_frozen, preferred_element_type=jnp.float32)
    branch_s = jnp.dot(columns_c, piece_trainee, preferred_element_type=jnp.float32)
    branch_c = branch_c.reshape(SAMPLES, image_dev, WIDTH)
    branch_n = branch_n.reshape(SAMPLES, image_dev, WIDTH)
    branch_s = branch_s.reshape(SAMPLES, image_dev, WIDTH)
    velocity_c = head_out(branch_c, image_states, gate, scale, final_head)
    velocity_n = head_out(branch_n, image_states, gate, scale, final_head)
    target = velocity_n - (velocity_c - velocity_n)

    def student(branch):
        velocity_s = head_out(branch, image_states, gate, scale, final_head)
        return jnp.sum((velocity_s - target) ** 2) / SAMPLES

    loss_part, pull = jax.vjp(student, branch_s)
    (cotangent,) = pull(jnp.ones_like(loss_part))
    cotangent_samples = cotangent.astype(jnp.bfloat16)
    cotangent_rows = cotangent_samples.reshape(token_rows, WIDTH)
    columns = attention[0]
    return lax.psum_scatter(
        lax.dot_general(
            columns, cotangent_rows, (((0,), (0,)), ((), ())), preferred_element_type=jnp.float32
        ),
        "seq",
        scatter_dimension=0,
        tiled=True,
    )


def solution(mesh):
    return jax.shard_map(
        shards,
        mesh=mesh,
        in_specs=(
            P(None, "grp", None, "seq", None),
            P(None, None, "grp", None, "seq", None),
            P(None, "grp", None),
            P("grp"),
            P("grp", "seq", None),
            P("seq", None),
            P(("grp", "seq"), None),
            P(),
            P(),
        ),
        out_specs=P(("grp", "seq"), None),
        check_vma=False,
    )
```

profile of v0, /device:TPU:0, one launch (start us, length us, event | category | flops | bytes accessed | tf_op | source)
XLA Modules:
  0.0 544.9 jit_solution(13315047425198892459)
XLA Ops:
  7.3 2.2 copy.27
  11.4 7.4 %all-to-all-start.1 = ((bf16[4,64,32,128]{3,2,0,1:T(8,128)(2,1)}), bf16[4,64,32,128]{3,2,0,1:T(8,128)(2,1)}, u32[]{:S(2)}, u32[]{:S(2)}) async-start(bf16[4,64,32,128]{3,2,0,1:T(8,128)(2,1)} %copy.28), calls=%async_computation.1 | async-start | bytes 4194304 | tf_op jit(solution)/shard_map/all_to_all | solution.py:78
  18.9 2.4 copy.23
  21.3 2.0 copy.24
  23.3 49.5 %all-to-all-done.1 = bf16[4,64,32,128]{3,2,0,1:T(8,128)(2,1)} async-done(((bf16[4,64,32,128]{3,2,0,1:T(8,128)(2,1)}), bf16[4,64,32,128]{3,2,0,1:T(8,128)(2,1)}, u32[]{:S(2)}, u32[]{:S(2)}) %all-to-all-start.1) | async-done | bytes 2097184 | tf_op jit(solution)/shard_map/all_to_all | solution.py:78
  72.8 33.3 %all-to-all-start = ((bf16[3,64,56,128]{3,2,0,1:T(8,128)(2,1)}), bf16[3,64,56,128]{3,2,0,1:T(8,128)(2,1)}, u32[]{:S(2)}, u32[]{:S(2)}) async-start(bf16[3,64,56,128]{3,2,0,1:T(8,128)(2,1)} %copy.24), calls=%async_computation | async-start | bytes 5505024 | tf_op jit(solution)/shard_map/all_to_all | solution.py:77
  107.1 3.4 copy.30
  110.6 72.9 %all-to-all-done = bf16[3,64,56,128]{3,2,0,1:T(8,128)(2,1)} async-done(((bf16[3,64,56,128]{3,2,0,1:T(8,128)(2,1)}), bf16[3,64,56,128]{3,2,0,1:T(8,128)(2,1)}, u32[]{:S(2)}, u32[]{:S(2)}) %all-to-all-start) | async-done | bytes 2752544 | tf_op jit(solution)/shard_map/all_to_all | solution.py:77
  183.5 4.0 copy.26
  187.4 113.6 %while.23 = (s32[]{:T(128)}, bf16[4,2,896,128]{3,1,0,2:T(2,128)(2,1)}, s32[4]{0:T(128)S(1)}, bf16[3,4,896,128]{3,2,1,0:T(8,128)(2,1)}, pred[2,4,512]{2,1,0:T(4,1...) while((s32[]{:T(128)}, ...), condition=%wide.region_9.10_spmd, body=%wide.region_0.9_spmd.sunk | while | flops 447742848 | bytes 26686016 | solution.py:116
  193.9 19.6 %while.24 = (s32[]{:T(128)}, bf16[2,2,448,128]{3,2,1,0:T(8,128)(2,1)}, bf16[2,448,128]{2,1,0:T(8,128)(2,1)S(1)}, bf16[896,128]{1,0:T(8,128)(2,1)}, pred[1,1,512]...) while((s32[]{:T(128)}, ...), condition=%wide.region_8.8_spmd, body=%wide.region_1.7_spmd.sunk | while | flops 447742848 | bytes 22390328 | solution.py:113
  195.9 2.1 fusion.139
  205.7 2.1 fusion.139
  222.3 19.6 %while.24 = (s32[]{:T(128)}, bf16[2,2,448,128]{3,2,1,0:T(8,128)(2,1)}, bf16[2,448,128]{2,1,0:T(8,128)(2,1)S(1)}, bf16[896,128]{1,0:T(8,128)(2,1)}, pred[1,1,512]...) while((s32[]{:T(128)}, ...), condition=%wide.region_8.8_spmd, body=%wide.region_1.7_spmd.sunk | while | flops 447742848 | bytes 22390328 | solution.py:113
  224.3 2.1 fusion.139
  234.1 2.1 fusion.139
  250.7 19.6 %while.24 = (s32[]{:T(128)}, bf16[2,2,448,128]{3,2,1,0:T(8,128)(2,1)}, bf16[2,448,128]{2,1,0:T(8,128)(2,1)S(1)}, bf16[896,128]{1,0:T(8,128)(2,1)}, pred[1,1,512]...) while((s32[]{:T(128)}, ...), condition=%wide.region_8.8_spmd, body=%wide.region_1.7_spmd.sunk | while | flops 447742848 | bytes 22390328 | solution.py:113
  252.7 2.1 fusion.139
  262.6 2.1 fusion.139
  279.1 19.6 %while.24 = (s32[]{:T(128)}, bf16[2,2,448,128]{3,2,1,0:T(8,128)(2,1)}, bf16[2,448,128]{2,1,0:T(8,128)(2,1)S(1)}, bf16[896,128]{1,0:T(8,128)(2,1)}, pred[1,1,512]...) while((s32[]{:T(128)}, ...), condition=%wide.region_8.8_spmd, body=%wide.region_1.7_spmd.sunk | while | flops 447742848 | bytes 22390328 | solution.py:113
  281.1 2.1 fusion.139
  291.0 2.1 fusion.139
  301.1 27.2 %all-to-all-start.2 = ((bf16[2,4,896,128]{3,0,1,2:T(2,128)(2,1)}), bf16[2,4,896,128]{3,0,1,2:T(2,128)(2,1)}, u32[]{:S(2)}, u32[]{:S(2)}) async-start(bf16[2,4,896,128]{3,0,1,2:T(2,128)(2,1)} %bitcast.168), calls=%async_computation.2 | async-start | bytes 3670016 | tf_op jit(solution)/shard_map/all_to_all | solution.py:119
  329.4 35.5 %all-to-all-done.2 = bf16[2,4,896,128]{3,0,1,2:T(2,128)(2,1)} async-done(((bf16[2,4,896,128]{3,0,1,2:T(2,128)(2,1)}), bf16[2,4,896,128]{3,0,1,2:T(2,128)(2,1)}, u32[]{:S(2)}, u32[]{:S(2)}) %all-to-all-start.2) | async-done | bytes 1835040 | tf_op jit(solution)/shard_map/all_to_all | solution.py:119
  364.9 2.7 copy.44
  370.1 2.2 dot_general.69
  372.4 4.9 multiply_reduce_fusion.4
  377.3 5.0 multiply_reduce_fusion.3
  382.7 2.8 multiply_reduce_fusion.2
  386.4 3.4 multiply_reduce_fusion.1
  391.6 6.4 %fusion.70 = f32[2048,1536]{1,0:T(8,128)} fusion(bf16[224,1536]{1,0:T(8,128)(2,1)S(1)} %bitcast.167, bf16[28,8,16,128]{3,2,1,0:T(8,128)(2,1)S(1)} %bitcast.164), kind=kOutput, calls=%fused_computation.90 | convolution fusion | flops 1409286144 | bytes 14188544 | tf_op jit(solution)/shard_map/dot_general | solution.py:153
  398.0 140.3 %reduce-scatter.2.cloned.1.call-done = f32[128,1536]{1,0:T(8,128)} async-done(((f32[2048,1536]{1,0:T(8,128)}), f32[128,1536]{1,0:T(8,128)}) %reduce-scatter.2.cloned.1.call-update) | async-done | bytes 786448 | tf_op jit(solution)/shard_map/reduce_scatter | solution.py:152
  (297 shorter events, 98.3 us)
Async XLA Ops:
  6.5 322.1 %copy-start = (bf16[256,3072]{1,0:T(8,128)(2,1)S(1)}, bf16[256,3072]{1,0:T(8,128)(2,1)}, u32[]{:S(2)}) copy-start(bf16[256,3072]{1,0:T(8,128)(2,1)} %param.20) | copy-start | bytes 4718596
  6.5 365.8 %all-gather.3.cloned.1.call-start = ((), (), s32[]{:S(2)}) async-start(), calls=%async_computation.4 | async-start | bytes 6684672 | tf_op jit(solution)/shard_map/all_gather | solution.py:130
  11.4 61.4 %all-to-all-start.1 = ((bf16[4,64,32,128]{3,2,0,1:T(8,128)(2,1)}), bf16[4,64,32,128]{3,2,0,1:T(8,128)(2,1)}, u32[]{:S(2)}, u32[]{:S(2)}) async-start(bf16[4,64,32,128]{3,2,0,1:T(8,128)(2,1)} %copy.28), calls=%async_computation.1 | async-start | bytes 4194304 | tf_op jit(solution)/shard_map/all_to_all | solution.py:78
  23.3 83.6 %copy-start.15 = (s32[2,4,512]{2,1,0:T(4,128)S(1)}, s32[2,4,512]{2,1,0:T(4,128)}, u32[]{:S(2)}) copy-start(s32[2,4,512]{2,1,0:T(4,128)} %param.15) | copy-start | bytes 49156
  72.8 110.7 %all-to-all-start = ((bf16[3,64,56,128]{3,2,0,1:T(8,128)(2,1)}), bf16[3,64,56,128]{3,2,0,1:T(8,128)(2,1)}, u32[]{:S(2)}, u32[]{:S(2)}) async-start(bf16[3,64,56,128]{3,2,0,1:T(8,128)(2,1)} %copy.24), calls=%async_computation | async-start | bytes 5505024 | tf_op jit(solution)/shard_map/all_to_all | solution.py:77
  106.1 271.1 %all-gather.5.cloned.1.call-start = ((), (), s32[]{:S(2)}) async-start(), calls=%async_computation.5 | async-start | bytes 6684672 | tf_op jit(solution)/shard_map/all_gather | solution.py:129
  187.4 2.5 copy-start.17
  187.4 6.4 %copy-start.11 = (pred[2,4,512]{2,1,0:T(4,128)(4,1)}, pred[2,4,512]{2,1,0:T(4,128)(4,1)S(1)}, u32[]{:S(2)}) copy-start(pred[2,4,512]{2,1,0:T(4,128)(4,1)S(1)} %get-tuple-element.467) | copy-start | bytes 12292 | tf_op jit(solution)/shard_map/while
  213.5 2.4 copy-start.12
  213.5 2.4 copy-start.18
  215.9 2.5 copy-start.17
  215.9 6.4 %copy-start.11 = (pred[2,4,512]{2,1,0:T(4,128)(4,1)}, pred[2,4,512]{2,1,0:T(4,128)(4,1)S(1)}, u32[]{:S(2)}) copy-start(pred[2,4,512]{2,1,0:T(4,128)(4,1)S(1)} %get-tuple-element.467) | copy-start | bytes 12292 | tf_op jit(solution)/shard_map/while
  229.4 1.2 copy-start.7
  241.9 2.4 copy-start.12
  241.9 2.4 copy-start.18
  244.3 2.5 copy-start.17
  244.3 6.4 %copy-start.11 = (pred[2,4,512]{2,1,0:T(4,128)(4,1)}, pred[2,4,512]{2,1,0:T(4,128)(4,1)S(1)}, u32[]{:S(2)}) copy-start(pred[2,4,512]{2,1,0:T(4,128)(4,1)S(1)} %get-tuple-element.467) | copy-start | bytes 12292 | tf_op jit(solution)/shard_map/while
  270.3 2.4 copy-start.12
  270.3 2.4 copy-start.18
  272.7 2.5 copy-start.17
  272.7 6.4 %copy-start.11 = (pred[2,4,512]{2,1,0:T(4,128)(4,1)}, pred[2,4,512]{2,1,0:T(4,128)(4,1)S(1)}, u32[]{:S(2)}) copy-start(pred[2,4,512]{2,1,0:T(4,128)(4,1)S(1)} %get-tuple-element.467) | copy-start | bytes 12292 | tf_op jit(solution)/shard_map/while
  298.7 2.4 copy-start.12
  298.7 2.4 copy-start.18
  301.1 27.4 %copy-start.16 = (s32[4]{0:T(128)S(1)}, s32[4]{0:T(128)}, u32[]{:S(2)}) copy-start(s32[4]{0:T(128)} %param.16) | copy-start | bytes 52
  301.1 63.8 %all-to-all-start.2 = ((bf16[2,4,896,128]{3,0,1,2:T(2,128)(2,1)}), bf16[2,4,896,128]{3,0,1,2:T(2,128)(2,1)}, u32[]{:S(2)}, u32[]{:S(2)}) async-start(bf16[2,4,896,128]{3,0,1,2:T(2,128)(2,1)} %bitcast.168), calls=%async_computation.2 | async-start | bytes 3670016 | tf_op jit(solution)/shard_map/all_to_all | solution.py:119
  328.2 210.1 %reduce-scatter.2.cloned.1.call-start = ((), (), s32[]{:S(2)}) async-start(), calls=%async_computation.6 | async-start | bytes 13369344 | tf_op jit(solution)/shard_map/reduce_scatter | solution.py:152
  368.8 3.6 copy-start.5
  377.3 5.1 copy-start.10
  377.3 5.3 copy-start.13
  377.3 5.4 copy-start.14
  382.7 2.9 copy-start.9
  389.8 1.8 copy-start.6
  (47 other events, 49.0 us)
Sparse Core Ops, SparseCore 0:
  9.6 98.0 all-gather.2
  110.0 94.7 all-gather.4
  398.2 140.1 reduce-scatter.1
where the time goes:
time: 547 us; the launch traced here: 545 us
  waiting for transfers between devices  300 us (55%)
  matrix products  71 us (13%)
  starting transfers between devices  68.2 us (12%)
  local copies, waits for them, and re-layouts  63.1 us (12%)
  other arithmetic  20.9 us (4%)
  between operations  13.3 us (2%)
  loops' own time  8.68 us (2%)
    reduce_scatter x1, waiting for transfers between devices, shards(): lax.psum_scatter(lax.dot_general(columns, cotangent_rows, (((0,), (0,)),...  140 us
    all_to_all x1, waiting for transfers between devices, shards(): lax.all_to_all(image_local, 'seq', split_axis=1, concat_axis=2, tiled=True)  72.9 us
    all_to_all x1, waiting for transfers between devices, shards(): lax.all_to_all(text_local, 'seq', split_axis=1, concat_axis=2, tiled=True)  49.5 us
    all_to_all x1, waiting for transfers between devices, shards(): lax.all_to_all(both_passes, 'seq', split_axis=2, concat_axis=1, tiled=True)  35.5 us
    all_to_all x1, starting transfers between devices, shards(): lax.all_to_all(image_local, 'seq', split_axis=1, concat_axis=2, tiled=True)  33.3 us
    all_to_all x1, starting transfers between devices, shards(): lax.all_to_all(both_passes, 'seq', split_axis=2, concat_axis=1, tiled=True)  27.2 us
    dot_general x16, matrix products, text_finish(): jnp.dot(queries, text_keys.T, preferred_element_type=jnp.float32) * factor  25.9 us
    while x128, local copies, waits for them, and re-layouts  12.1 us
  transfers between devices with their start and end apart: 6, of which 4 were waited for; matrix products, arithmetic and copies ran while one was open for 22% of the time, Pallas kernels for 0%

commit v1 on v0

--- a/solution.py
+++ b/solution.py
@@ -9,6 +9,12 @@
 HEAD_DIM = 128
 WIDTH = 1536
 TIME_DIM = 256
+
+
+def swap_blocks(x, axis, split, join):
+    cells = jnp.split(x, lax.axis_size(axis), axis=split)
+    got = lax.all_to_all(jnp.stack(cells), axis, 0, 0)
+    return jnp.concatenate(got, axis=join)
 
 
 def image_block(queries, image_keys, image_values):
@@ -116,7 +122,7 @@
     both_passes = lax.map(joint_item, jnp.arange(owned_count, dtype=jnp.int32)).transpose(
         1, 0, 2, 3
     )
-    returned = lax.all_to_all(both_passes, "seq", split_axis=2, concat_axis=1, tiled=True)
+    returned = swap_blocks(both_passes, "seq", 2, 1)
     attention = returned.reshape(2, HEADS, SAMPLES, image_dev, HEAD_DIM).transpose(0, 2, 3, 1, 4)
     attention = attention.reshape(2, token_rows, HEADS * HEAD_DIM)
     half_dim = TIME_DIM // 2

time: 547 us -> 555 us (1.015)
  local copies, waits for them, and re-layouts: 63.1 us -> 74.5 us
    unnamed x20 -> x39, local copies, waits for them, and re-layouts: 5 us -> 22.1 us
    dot_general x8, matrix products: 3.86 us -> 11.5 us  [image_block(): jnp.dot(image_exp.astype(jnp.bfloat16), image_values, preferred_element_t...]
    while x128 -> x112, local copies, waits for them, and re-layouts: 12.1 us -> 8.65 us
  transfers between devices with their start and end apart: 6 -> 6, of which waited for: 4 -> 4; matrix products, arithmetic and copies ran while one was open for 22% -> 24% of each run, Pallas kernels for 0% -> 0%
where the time goes in v1:
time: 555 us; the launch traced here: 553 us
  waiting for transfers between devices  299 us (54%)
  local copies, waits for them, and re-layouts  74.5 us (13%)
  matrix products  73.2 us (13%)
  starting transfers between devices  68.1 us (12%)
  other arithmetic  16.3 us (3%)
  between operations  13.3 us (2%)
  loops' own time  8.48 us (2%)
    reduce_scatter x1, waiting for transfers between devices, shards(): lax.psum_scatter(lax.dot_general(columns, cotangent_rows, (((0,), (0,)),...  140 us
    all_to_all x1, waiting for transfers between devices, shards(): lax.all_to_all(image_local, 'seq', split_axis=1, concat_axis=2, tiled=True)  72.9 us
    all_to_all x1, waiting for transfers between devices, shards(): lax.all_to_all(text_local, 'seq', split_axis=1, concat_axis=2, tiled=True)  49.5 us
    all_to_all x1, waiting for transfers between devices, swap_blocks(): got = lax.all_to_all(jnp.stack(cells), axis, 0, 0)  35.4 us
    all_to_all x1, starting transfers between devices, shards(): lax.all_to_all(image_local, 'seq', split_axis=1, concat_axis=2, tiled=True)  33.3 us
    all_to_all x1, starting transfers between devices, swap_blocks(): got = lax.all_to_all(jnp.stack(cells), axis, 0, 0)  27.1 us
    unnamed x39, local copies, waits for them, and re-layouts  22.1 us
    dot_general x16, matrix products, text_finish(): jnp.dot(queries, text_keys.T, preferred_element_type=jnp.float32) * factor  20.6 us
  transfers between devices with their start and end apart: 6, of which 4 were waited for; matrix products, arithmetic and copies ran while one was open for 24% of the time, Pallas kernels for 0%

profile of v1, /device:TPU:0, one launch (start us, length us, event | category | flops | bytes accessed | tf_op | source)
XLA Modules:
  0.0 553.3 jit_solution(9149514357397811513)
XLA Ops:
  7.3 2.2 copy.32
  9.5 2.0 copy.33
  11.4 7.4 %all-to-all-start.1 = ((bf16[4,64,32,128]{3,2,0,1:T(8,128)(2,1)}), bf16[4,64,32,128]{3,2,0,1:T(8,128)(2,1)}, u32[]{:S(2)}, u32[]{:S(2)}) async-start(bf16[4,64,32,128]{3,2,0,1:T(8,128)(2,1)} %copy.33), calls=%async_computation.1 | async-start | bytes 4194304 | tf_op jit(solution)/shard_map/all_to_all | solution.py:84
  18.9 2.4 copy.28
  21.3 2.0 copy.29
  23.3 49.5 %all-to-all-done.1 = bf16[4,64,32,128]{3,2,0,1:T(8,128)(2,1)} async-done(((bf16[4,64,32,128]{3,2,0,1:T(8,128)(2,1)}), bf16[4,64,32,128]{3,2,0,1:T(8,128)(2,1)}, u32[]{:S(2)}, u32[]{:S(2)}) %all-to-all-start.1) | async-done | bytes 2097184 | tf_op jit(solution)/shard_map/all_to_all | solution.py:84
  72.8 33.3 %all-to-all-start = ((bf16[3,64,56,128]{3,2,0,1:T(8,128)(2,1)}), bf16[3,64,56,128]{3,2,0,1:T(8,128)(2,1)}, u32[]{:S(2)}, u32[]{:S(2)}) async-start(bf16[3,64,56,128]{3,2,0,1:T(8,128)(2,1)} %copy.29), calls=%async_computation | async-start | bytes 5505024 | tf_op jit(solution)/shard_map/all_to_all | solution.py:83
  107.2 3.4 copy.35
  110.6 72.9 %all-to-all-done = bf16[3,64,56,128]{3,2,0,1:T(8,128)(2,1)} async-done(((bf16[3,64,56,128]{3,2,0,1:T(8,128)(2,1)}), bf16[3,64,56,128]{3,2,0,1:T(8,128)(2,1)}, u32[]{:S(2)}, u32[]{:S(2)}) %all-to-all-start) | async-done | bytes 2752544 | tf_op jit(solution)/shard_map/all_to_all | solution.py:83
  183.5 4.0 copy.31
  187.5 105.8 %while.23 = (s32[]{:T(128)}, bf16[4,2,896,128]{3,2,1,0:T(8,128)(2,1)}, s32[4]{0:T(128)S(1)}, bf16[3,4,896,128]{3,2,1,0:T(8,128)(2,1)}, pred[2,4,512]{2,1,0:T(4,1...) while((s32[]{:T(128)}, ...), condition=%wide.region_9.10_spmd, body=%wide.region_0.9_spmd.sunk | while | flops 447742848 | bytes 25767992 | solution.py:122
  190.0 2.0 dynamic-slice_bitcast_fusion.3
  192.0 1.9 constant_dynamic-slice_fusion.10
  193.9 18.2 %while.24 = (s32[]{:T(128)}, bf16[2,2,448,128]{3,2,1,0:T(8,128)(2,1)}, bf16[2,448,128]{2,1,0:T(8,128)(2,1)S(1)}, bf16[896,128]{1,0:T(8,128)(2,1)}, pred[1,1,512]...) while((s32[]{:T(128)}, ...), condition=%wide.region_8.8_spmd, body=%wide.region_1.7_spmd.sunk | while | flops 447742848 | bytes 21472804 | solution.py:119
  216.5 2.0 dynamic-slice_bitcast_fusion.3
  218.5 1.9 constant_dynamic-slice_fusion.10
  220.4 18.1 %while.24 = (s32[]{:T(128)}, bf16[2,2,448,128]{3,2,1,0:T(8,128)(2,1)}, bf16[2,448,128]{2,1,0:T(8,128)(2,1)S(1)}, bf16[896,128]{1,0:T(8,128)(2,1)}, pred[1,1,512]...) while((s32[]{:T(128)}, ...), condition=%wide.region_8.8_spmd, body=%wide.region_1.7_spmd.sunk | while | flops 447742848 | bytes 21472804 | solution.py:119
  242.9 2.0 dynamic-slice_bitcast_fusion.3
  244.9 1.9 constant_dynamic-slice_fusion.10
  246.8 18.1 %while.24 = (s32[]{:T(128)}, bf16[2,2,448,128]{3,2,1,0:T(8,128)(2,1)}, bf16[2,448,128]{2,1,0:T(8,128)(2,1)S(1)}, bf16[896,128]{1,0:T(8,128)(2,1)}, pred[1,1,512]...) while((s32[]{:T(128)}, ...), condition=%wide.region_8.8_spmd, body=%wide.region_1.7_spmd.sunk | while | flops 447742848 | bytes 21472804 | solution.py:119
  269.4 2.0 dynamic-slice_bitcast_fusion.3
  271.4 1.9 constant_dynamic-slice_fusion.10
  273.2 18.1 %while.24 = (s32[]{:T(128)}, bf16[2,2,448,128]{3,2,1,0:T(8,128)(2,1)}, bf16[2,448,128]{2,1,0:T(8,128)(2,1)S(1)}, bf16[896,128]{1,0:T(8,128)(2,1)}, pred[1,1,512]...) while((s32[]{:T(128)}, ...), condition=%wide.region_8.8_spmd, body=%wide.region_1.7_spmd.sunk | while | flops 447742848 | bytes 21472804 | solution.py:119
  311.1 27.1 %all-to-all-start.2 = ((bf16[16,2,4,56,128]{4,3,1,2,0:T(8,128)(2,1)}), bf16[16,2,4,56,128]{4,3,1,2,0:T(8,128)(2,1)S(1)}, u32[]{:S(2)}, u32[]{:S(2)}) async-start(bf16[16,2,4,56,128]{4,3,1,2,0:T(8,128)(2,1)} %fusion.87), calls=%async_computation.2 | async-start | bytes 3670016 | tf_op jit(solution)/shard_map/all_to_all | solution.py:16
  339.3 35.4 %all-to-all-done.2 = bf16[16,2,4,56,128]{4,3,1,2,0:T(8,128)(2,1)S(1)} async-done(((bf16[16,2,4,56,128]{4,3,1,2,0:T(8,128)(2,1)}), bf16[16,2,4,56,128]{4,3,1,2,0:T(8,128)(2,1)S(1)}, u32[]{:S(2)}, u32[]{:S(2)}) %all-to-all-start.2) | async-done | bytes 1835040 | tf_op jit(solution)/shard_map/all_to_all | solution.py:16
  378.8 2.2 dot_general.69
  381.0 4.9 multiply_reduce_fusion.4
  386.0 5.0 multiply_reduce_fusion.3
  391.4 2.8 multiply_reduce_fusion.2
  395.0 3.4 multiply_reduce_fusion.1
  400.2 6.4 %fusion.70 = f32[2048,1536]{1,0:T(8,128)} fusion(bf16[224,1536]{1,0:T(8,128)(2,1)S(1)} %bitcast.228, bf16[28,8,16,128]{3,2,1,0:T(8,128)(2,1)S(1)} %bitcast.225), kind=kOutput, calls=%fused_computation.89 | convolution fusion | flops 1409286144 | bytes 14188544 | tf_op jit(solution)/shard_map/dot_general | solution.py:159
  406.6 140.1 %reduce-scatter.2.cloned.1.call-done = f32[128,1536]{1,0:T(8,128)} async-done(((f32[2048,1536]{1,0:T(8,128)}), f32[128,1536]{1,0:T(8,128)}) %reduce-scatter.2.cloned.1.call-update) | async-done | bytes 786448 | tf_op jit(solution)/shard_map/reduce_scatter | solution.py:158
  (302 shorter events, 109.6 us)
Async XLA Ops:
  6.5 332.0 %copy-start = (bf16[256,3072]{1,0:T(8,128)(2,1)S(1)}, bf16[256,3072]{1,0:T(8,128)(2,1)}, u32[]{:S(2)}) copy-start(bf16[256,3072]{1,0:T(8,128)(2,1)} %param.20) | copy-start | bytes 4718596
  6.5 374.5 %all-gather.3.cloned.1.call-start = ((), (), s32[]{:S(2)}) async-start(), calls=%async_computation.4 | async-start | bytes 6684672 | tf_op jit(solution)/shard_map/all_gather | solution.py:136
  11.4 61.4 %all-to-all-start.1 = ((bf16[4,64,32,128]{3,2,0,1:T(8,128)(2,1)}), bf16[4,64,32,128]{3,2,0,1:T(8,128)(2,1)}, u32[]{:S(2)}, u32[]{:S(2)}) async-start(bf16[4,64,32,128]{3,2,0,1:T(8,128)(2,1)} %copy.33), calls=%async_computation.1 | async-start | bytes 4194304 | tf_op jit(solution)/shard_map/all_to_all | solution.py:84
  23.3 83.6 %copy-start.16 = (s32[2,4,512]{2,1,0:T(4,128)S(1)}, s32[2,4,512]{2,1,0:T(4,128)}, u32[]{:S(2)}) copy-start(s32[2,4,512]{2,1,0:T(4,128)} %param.15) | copy-start | bytes 49156
  72.8 110.7 %all-to-all-start = ((bf16[3,64,56,128]{3,2,0,1:T(8,128)(2,1)}), bf16[3,64,56,128]{3,2,0,1:T(8,128)(2,1)}, u32[]{:S(2)}, u32[]{:S(2)}) async-start(bf16[3,64,56,128]{3,2,0,1:T(8,128)(2,1)} %copy.29), calls=%async_computation | async-start | bytes 5505024 | tf_op jit(solution)/shard_map/all_to_all | solution.py:83
  106.2 279.8 %all-gather.5.cloned.1.call-start = ((), (), s32[]{:S(2)}) async-start(), calls=%async_computation.5 | async-start | bytes 6684672 | tf_op jit(solution)/shard_map/all_gather | solution.py:135
  187.5 1.9 copy-start.18
  187.5 4.5 copy-start.12
  197.1 2.9 copy-start.1
  206.2 2.8 copy-start.1
  213.9 1.9 copy-start.18
  213.9 4.5 copy-start.12
  223.6 2.8 copy-start.1
  232.7 2.8 copy-start.1
  238.5 1.9 copy-start.19
  240.4 1.9 copy-start.18
  240.4 4.5 copy-start.12
  250.0 2.8 copy-start.1
  259.1 2.8 copy-start.1
  266.8 1.9 copy-start.18
  266.8 4.5 copy-start.12
  276.5 2.8 copy-start.1
  285.5 2.8 copy-start.1
  293.3 12.6 %copy-start.10 = (bf16[4,2,896,128]{3,2,1,0:T(8,128)(2,1)S(1)}, bf16[4,2,896,128]{3,2,1,0:T(8,128)(2,1)}, u32[]{:S(2)}) copy-start(bf16[4,2,896,128]{3,2,1,0:T(8,128)(2,1)} %get-tuple-element.153) | copy-start | bytes 5505028
  311.1 27.3 %copy-start.17 = (s32[4]{0:T(128)S(1)}, s32[4]{0:T(128)}, u32[]{:S(2)}) copy-start(s32[4]{0:T(128)} %param.16) | copy-start | bytes 52
  311.1 63.6 %all-to-all-start.2 = ((bf16[16,2,4,56,128]{4,3,1,2,0:T(8,128)(2,1)}), bf16[16,2,4,56,128]{4,3,1,2,0:T(8,128)(2,1)S(1)}, u32[]{:S(2)}, u32[]{:S(2)}) async-start(bf16[16,2,4,56,128]{4,3,1,2,0:T(8,128)(2,1)} %fusion.87), calls=%async_computation.2 | async-start | bytes 3670016 | tf_op jit(solution)/shard_map/all_to_all | solution.py:16
  338.1 208.6 %reduce-scatter.2.cloned.1.call-start = ((), (), s32[]{:S(2)}) async-start(), calls=%async_computation.6 | async-start | bytes 13369344 | tf_op jit(solution)/shard_map/reduce_scatter | solution.py:158
  376.1 2.7 copy-start.4
  385.9 5.1 copy-start.11
  385.9 5.3 copy-start.14
  386.0 5.4 copy-start.15
  391.4 2.8 copy-start.9
  (41 other events, 48.1 us)
Sparse Core Ops, SparseCore 0:
  9.6 98.0 all-gather.2
  110.0 94.8 all-gather.4
  406.8 139.9 reduce-scatter.1
